TPU v7x, 128 devices: a whole 4x4x4 slice. The times are simulated.
128 devices in a mesh: dom: 16 (over y_lo, z, core), rep: 8 (over y_hi, x).
Axes of the slice: x: 4, y: 4 (y_hi: 2, y_lo: 2; y = y_hi * 2 + y_lo), z: 4, core: 2. Of those that a mesh axis runs over, the one named last changes fastest.
Arguments:
- node_features: bfloat16 [65536, 256], P(('dom', 'rep')), may hold values from -6 to 6
- weight: bfloat16 [256, 256], replicated, may hold values from -0.375 to 0.375
- cotangent: bfloat16 [65536, 256], P(('dom', 'rep')), may hold values from -6 to 6
- tile_row: int32 [16, 8, 512], P('dom', 'rep'), may hold values from 0 to 31
- tile_col: int32 [16, 8, 512], P('dom', 'rep'), may hold values from 0 to 63
- tile_values: bfloat16 [16, 8, 512, 128, 128], P('dom', 'rep'), may hold values from -0.0625 to 0.0625
- tile_count: int32 [16, 8], P('dom', 'rep'), may hold values from 128 to 512, as said below
Outputs:
- output: bfloat16 [65536, 256], P(('dom', 'rep'))
- grad_features: bfloat16 [65536, 256], P(('dom', 'rep'))
- grad_weight: float32 [256, 256], replicated
Inputs may be any that keep to these rules, and one draw needn't show every extreme that they name: Live slots are the first tile_count slots of each device's list; some device has all 512 slots live.
All inputs are finite; a program needn't handle non-finite values.
Results may differ from a plain program's by a relative error of at most 0.0061.
Values may be sent and summed in bfloat16 or wider, within the bound.
No kernel may reach another device: no remote copies, remote signals or barrier semaphores. Data moves between devices by JAX's collectives and lax.ppermute only.
A program may use at most 192 MiB of HBM per device.

v0:
```python
import jax
import jax.numpy as jnp
from jax import lax
from jax.sharding import PartitionSpec as P


def silu_slope(summed):
    sig = jax.nn.sigmoid(summed)
    return sig * (1.0 + summed * (1.0 - sig))


def tile_products(values, pick_index, place_index, active, source, out_blocks, flipped):
    slots = values.shape[0]
    feature_width = source.shape[2]
    per_turn = min(slots, 128)
    pattern = "tba,tbf->taf" if flipped else "tab,tbf->taf"

    def accumulate(turn_index, summed):
        first_slot = turn_index * per_turn
        block_values = lax.dynamic_slice_in_dim(values, first_slot, per_turn, 0)
        picks = lax.dynamic_slice_in_dim(pick_index, first_slot, per_turn, 0)
        picked = jnp.take(source, picks, axis=0)
        products = jnp.einsum(pattern, block_values, picked, preferred_element_type=jnp.float32)
        places = lax.dynamic_slice_in_dim(place_index, first_slot, per_turn, 0)
        enabled = lax.dynamic_slice_in_dim(active, first_slot, per_turn, 0)
        products = products * enabled.astype(jnp.float32)[:, None, None]
        return summed.at[places].add(products)

    initial = jnp.zeros((out_blocks, 128, feature_width), jnp.float32)
    summed = lax.fori_loop(0, slots // per_turn, accumulate, initial)
    return summed.reshape(out_blocks * 128, feature_width)


def body(node_features, weight, cotangent, tile_row, tile_col, tile_values, tile_count):
    rows_here = node_features.shape[0]
    feature_width = weight.shape[0]
    dom_size = lax.axis_size("dom")
    rep_size = lax.axis_size("rep")
    slots = tile_row.shape[2]
    row_index = tile_row.reshape(slots)
    col_index = tile_col.reshape(slots)
    values = tile_values.reshape(slots, 128, 128)
    active = lax.broadcasted_iota(jnp.int32, (slots,), 0) < tile_count.reshape(())
    projected = jnp.dot(node_features, weight, preferred_element_type=jnp.float32).astype(
        jnp.bfloat16
    )
    gathered = lax.all_gather(projected, "dom", axis=0, tiled=True)
    source = gathered.reshape(-1, 128, feature_width)
    part_blocks = rep_size * rows_here // 128
    partial_value = tile_products(values, col_index, row_index, active, source, part_blocks, False)
    summed = lax.psum_scatter(partial_value, "rep", scatter_dimension=0, tiled=True)
    output = jax.nn.silu(summed).astype(jnp.bfloat16)
    grad_own = (cotangent.astype(jnp.float32) * silu_slope(summed)).astype(jnp.bfloat16)
    grad_block = lax.all_gather(grad_own, "rep", axis=0, tiled=True)
    back_blocks = dom_size * rows_here // 128
    back_partial = tile_products(
        values,
        row_index,
        col_index,
        active,
        grad_block.reshape(-1, 128, feature_width),
        back_blocks,
        True,
    )
    grad_projected = lax.psum_scatter(back_partial, "dom", scatter_dimension=0, tiled=True).astype(
        jnp.bfloat16
    )
    grad_features = jnp.dot(grad_projected, weight.T, preferred_element_type=jnp.float32).astype(
        jnp.bfloat16
    )
    local_weight = jnp.dot(node_features.T, grad_projected, preferred_element_type=jnp.float32)
    grad_weight = lax.psum(local_weight, ("dom", "rep"))
    return (output, grad_features, grad_weight)


def solution(mesh):
    placed = (
        P(("dom", "rep"), None),
        P(),
        P(("dom", "rep"), None),
        P("dom", "rep", None),
        P("dom", "rep", None),
        P("dom", "rep", None, None, None),
        P("dom", "rep"),
    )
    return jax.shard_map(
        body,
        mesh=mesh,
        in_specs=placed,
        out_specs=(P(("dom", "rep"), None), P(("dom", "rep"), None), P()),
        check_vma=False,
    )
```

profile of v0, /device:TPU:1, one launch (start us, length us, event | category | flops | bytes accessed | tf_op | source)
XLA Modules:
  0.0 908.0 jit_solution(10777865380881318707)
XLA Ops:
  10.7 40.7 %all-gather.3.cloned.1.call-done = bf16[8192,256]{1,0:T(8,128)(2,1)} async-done(((bf16[512,256]{1,0:T(8,128)(2,1)}), bf16[8192,256]{1,0:T(8,128)(2,1)}) %all-gather.3.cloned.1.call-update) | async-done | bytes 4194320 | tf_op jit(solution)/shard_map/all_gather | solution.py:47
  53.8 244.2 %while.26 = (s32[]{:T(128)}, f32[32,128,256]{2,1,0:T(8,128)}, s32[512]{0:T(512)}, bf16[512,128,128]{2,1,0:T(8,128)(2,1)}, s32[512]{0:T(512)}, /*index=5*/bf16[64...) while((s32[]{:T(128)}, f32[32,128,256]{2,1,0:T(8,128)}, ...), condition=%wide.region_2.3_spmd, body=%wide.region_0.2_spmd.sunk | while | flops 1086327040 | bytes 96478248 | solution.py:30
  54.6 8.8 gather_fusion
  63.4 12.8 %convolution_multiply_fusion.4 = f32[128,128,256]{2,1,0:T(8,128)} fusion(f32[128]{0:T(128)S(1)} %get-tuple-element.384, bf16[128,128,256]{2,1,0:T(8,128)(2,1)} %gather_fusion, pred[128]{0:T(512)(128)(4,1)S(1)} %get-tuple-element.386, bf16[512,128,128]{2,1,0:T(8,128)(2,1)} %get-tuple-element.422, s32[]{:T(128)S(6)} %select_n.85), kind=kOutput, calls=%fused_computation.4.clone.1 | convolution fusion | flops 1082130432 | bytes 29360772 | tf_op jit(solution)/shard_map/while/body/eval_jaxpr/tab,tbf->taf/dot_general | solution.py:23
  76.9 38.1 %scatter_fusion = f32[32,128,256]{2,1,0:T(8,128)} fusion(f32[32,128,256]{2,1,0:T(8,128)} %get-tuple-element.409, s32[128]{0:T(128)S(1)} %compare_select_fusion.8, f32[128,128,256]{2,1,0:T(8,128)} %convolution_multiply_fusion.4), kind=kCustom, calls=%fused_computation.2.clone.1 | custom fusion | flops 4194304 | bytes 50332160 | tf_op jit(solution)/shard_map/while/body/eval_jaxpr/scatter-add | solution.py:27
  115.8 8.8 gather_fusion
  124.5 12.8 %convolution_multiply_fusion.4 = f32[128,128,256]{2,1,0:T(8,128)} fusion(f32[128]{0:T(128)S(1)} %get-tuple-element.384, bf16[128,128,256]{2,1,0:T(8,128)(2,1)} %gather_fusion, pred[128]{0:T(512)(128)(4,1)S(1)} %get-tuple-element.386, bf16[512,128,128]{2,1,0:T(8,128)(2,1)} %get-tuple-element.422, s32[]{:T(128)S(6)} %select_n.85), kind=kOutput, calls=%fused_computation.4.clone.1 | convolution fusion | flops 1082130432 | bytes 29360772 | tf_op jit(solution)/shard_map/while/body/eval_jaxpr/tab,tbf->taf/dot_general | solution.py:23
  138.1 38.1 %scatter_fusion = f32[32,128,256]{2,1,0:T(8,128)} fusion(f32[32,128,256]{2,1,0:T(8,128)} %get-tuple-element.409, s32[128]{0:T(128)S(1)} %compare_select_fusion.8, f32[128,128,256]{2,1,0:T(8,128)} %convolution_multiply_fusion.4), kind=kCustom, calls=%fused_computation.2.clone.1 | custom fusion | flops 4194304 | bytes 50332160 | tf_op jit(solution)/shard_map/while/body/eval_jaxpr/scatter-add | solution.py:27
  176.9 8.8 gather_fusion
  185.7 12.8 %convolution_multiply_fusion.4 = f32[128,128,256]{2,1,0:T(8,128)} fusion(f32[128]{0:T(128)S(1)} %get-tuple-element.384, bf16[128,128,256]{2,1,0:T(8,128)(2,1)} %gather_fusion, pred[128]{0:T(512)(128)(4,1)S(1)} %get-tuple-element.386, bf16[512,128,128]{2,1,0:T(8,128)(2,1)} %get-tuple-element.422, s32[]{:T(128)S(6)} %select_n.85), kind=kOutput, calls=%fused_computation.4.clone.1 | convolution fusion | flops 1082130432 | bytes 29360772 | tf_op jit(solution)/shard_map/while/body/eval_jaxpr/tab,tbf->taf/dot_general | solution.py:23
  199.3 37.7 %scatter_fusion = f32[32,128,256]{2,1,0:T(8,128)} fusion(f32[32,128,256]{2,1,0:T(8,128)} %get-tuple-element.409, s32[128]{0:T(128)S(1)} %compare_select_fusion.8, f32[128,128,256]{2,1,0:T(8,128)} %convolution_multiply_fusion.4), kind=kCustom, calls=%fused_computation.2.clone.1 | custom fusion | flops 4194304 | bytes 50332160 | tf_op jit(solution)/shard_map/while/body/eval_jaxpr/scatter-add | solution.py:27
  237.7 8.8 gather_fusion
  246.5 12.8 %convolution_multiply_fusion.4 = f32[128,128,256]{2,1,0:T(8,128)} fusion(f32[128]{0:T(128)S(1)} %get-tuple-element.384, bf16[128,128,256]{2,1,0:T(8,128)(2,1)} %gather_fusion, pred[128]{0:T(512)(128)(4,1)S(1)} %get-tuple-element.386, bf16[512,128,128]{2,1,0:T(8,128)(2,1)} %get-tuple-element.422, s32[]{:T(128)S(6)} %select_n.85), kind=kOutput, calls=%fused_computation.4.clone.1 | convolution fusion | flops 1082130432 | bytes 29360772 | tf_op jit(solution)/shard_map/while/body/eval_jaxpr/tab,tbf->taf/dot_general | solution.py:23
  260.1 37.9 %scatter_fusion = f32[32,128,256]{2,1,0:T(8,128)} fusion(f32[32,128,256]{2,1,0:T(8,128)} %get-tuple-element.409, s32[128]{0:T(128)S(1)} %compare_select_fusion.8, f32[128,128,256]{2,1,0:T(8,128)} %convolution_multiply_fusion.4), kind=kCustom, calls=%fused_computation.2.clone.1 | custom fusion | flops 4194304 | bytes 50332160 | tf_op jit(solution)/shard_map/while/body/eval_jaxpr/scatter-add | solution.py:27
  298.0 83.2 %reduce-scatter.3.cloned.1.call-done = f32[512,256]{1,0:T(8,128)} async-done(((f32[4096,256]{1,0:T(8,128)}), f32[512,256]{1,0:T(8,128)}) %reduce-scatter.3.cloned.1.call-update) | async-done | bytes 524304 | tf_op jit(solution)/shard_map/reduce_scatter | solution.py:51
  383.6 22.4 %copy.10 = bf16[1,1,512,128,128]{3,4,2,1,0:T(8,128)(2,1)} copy(bf16[1,1,512,128,128]{4,3,2,1,0:T(8,128)(2,1)} %bitcast.21) | data formatting | bytes 33554432 | tf_op args[5]
  406.0 31.9 %all-gather.5.cloned.1.call-done = bf16[4096,256]{1,0:T(8,128)(2,1)} async-done(((bf16[512,256]{1,0:T(8,128)(2,1)}), bf16[4096,256]{1,0:T(8,128)(2,1)}) %all-gather.5.cloned.1.call-update) | async-done | bytes 2097168 | tf_op jit(solution)/shard_map/all_gather | solution.py:54
  442.1 236.8 %while.27 = (s32[]{:T(128)}, f32[64,128,256]{2,1,0:T(8,128)}, s32[512]{0:T(512)}, bf16[512,128,128]{1,2,0:T(8,128)(2,1)}, s32[512]{0:T(512)}, /*index=5*/bf16[32...) while((s32[]{:T(128)}, f32[64,128,256]{2,1,0:T(8,128)}, ...), condition=%wide.region_6.7_spmd, body=%wide.region_4.6_spmd.sunk | while | flops 1086327040 | bytes 96478248 | solution.py:30
  442.9 6.6 gather_fusion.1
  449.5 12.8 %convolution_multiply_fusion.5 = f32[128,128,256]{2,1,0:T(8,128)} fusion(f32[128]{0:T(128)S(1)} %get-tuple-element.394, bf16[128,128,256]{2,1,0:T(8,128)(2,1)} %gather_fusion.1, pred[128]{0:T(512)(128)(4,1)S(1)} %get-tuple-element.396, bf16[512,128,128]{1,2,0:T(8,128)(2,1)} %get-tuple-element.455, s32[]{:T(128)S(6)} %select_n.88), kind=kOutput, calls=%fused_computation.16.clone.1 | convolution fusion | flops 1082130432 | bytes 29360772 | tf_op jit(solution)/shard_map/while/body/eval_jaxpr/tba,tbf->taf/dot_general | solution.py:23
  463.1 38.5 %scatter_fusion.1 = f32[64,128,256]{2,1,0:T(8,128)} fusion(f32[64,128,256]{2,1,0:T(8,128)} %get-tuple-element.442, s32[128]{0:T(128)S(1)} %compare_select_fusion.9, f32[128,128,256]{2,1,0:T(8,128)} %convolution_multiply_fusion.5), kind=kCustom, calls=%fused_computation.3.clone.1 | custom fusion | flops 4194304 | bytes 50332160 | tf_op jit(solution)/shard_map/while/body/eval_jaxpr/scatter-add | solution.py:27
  502.3 6.6 gather_fusion.1
  508.9 12.8 %convolution_multiply_fusion.5 = f32[128,128,256]{2,1,0:T(8,128)} fusion(f32[128]{0:T(128)S(1)} %get-tuple-element.394, bf16[128,128,256]{2,1,0:T(8,128)(2,1)} %gather_fusion.1, pred[128]{0:T(512)(128)(4,1)S(1)} %get-tuple-element.396, bf16[512,128,128]{1,2,0:T(8,128)(2,1)} %get-tuple-element.455, s32[]{:T(128)S(6)} %select_n.88), kind=kOutput, calls=%fused_computation.16.clone.1 | convolution fusion | flops 1082130432 | bytes 29360772 | tf_op jit(solution)/shard_map/while/body/eval_jaxpr/tba,tbf->taf/dot_general | solution.py:23
  522.5 38.1 %scatter_fusion.1 = f32[64,128,256]{2,1,0:T(8,128)} fusion(f32[64,128,256]{2,1,0:T(8,128)} %get-tuple-element.442, s32[128]{0:T(128)S(1)} %compare_select_fusion.9, f32[128,128,256]{2,1,0:T(8,128)} %convolution_multiply_fusion.5), kind=kCustom, calls=%fused_computation.3.clone.1 | custom fusion | flops 4194304 | bytes 50332160 | tf_op jit(solution)/shard_map/while/body/eval_jaxpr/scatter-add | solution.py:27
  561.3 6.6 gather_fusion.1
  567.9 12.8 %convolution_multiply_fusion.5 = f32[128,128,256]{2,1,0:T(8,128)} fusion(f32[128]{0:T(128)S(1)} %get-tuple-element.394, bf16[128,128,256]{2,1,0:T(8,128)(2,1)} %gather_fusion.1, pred[128]{0:T(512)(128)(4,1)S(1)} %get-tuple-element.396, bf16[512,128,128]{1,2,0:T(8,128)(2,1)} %get-tuple-element.455, s32[]{:T(128)S(6)} %select_n.88), kind=kOutput, calls=%fused_computation.16.clone.1 | convolution fusion | flops 1082130432 | bytes 29360772 | tf_op jit(solution)/shard_map/while/body/eval_jaxpr/tba,tbf->taf/dot_general | solution.py:23
  581.5 38.3 %scatter_fusion.1 = f32[64,128,256]{2,1,0:T(8,128)} fusion(f32[64,128,256]{2,1,0:T(8,128)} %get-tuple-element.442, s32[128]{0:T(128)S(1)} %compare_select_fusion.9, f32[128,128,256]{2,1,0:T(8,128)} %convolution_multiply_fusion.5), kind=kCustom, calls=%fused_computation.3.clone.1 | custom fusion | flops 4194304 | bytes 50332160 | tf_op jit(solution)/shard_map/while/body/eval_jaxpr/scatter-add | solution.py:27
  620.5 6.6 gather_fusion.1
  627.1 12.8 %convolution_multiply_fusion.5 = f32[128,128,256]{2,1,0:T(8,128)} fusion(f32[128]{0:T(128)S(1)} %get-tuple-element.394, bf16[128,128,256]{2,1,0:T(8,128)(2,1)} %gather_fusion.1, pred[128]{0:T(512)(128)(4,1)S(1)} %get-tuple-element.396, bf16[512,128,128]{1,2,0:T(8,128)(2,1)} %get-tuple-element.455, s32[]{:T(128)S(6)} %select_n.88), kind=kOutput, calls=%fused_computation.16.clone.1 | convolution fusion | flops 1082130432 | bytes 29360772 | tf_op jit(solution)/shard_map/while/body/eval_jaxpr/tba,tbf->taf/dot_general | solution.py:23
  640.7 38.3 %scatter_fusion.1 = f32[64,128,256]{2,1,0:T(8,128)} fusion(f32[64,128,256]{2,1,0:T(8,128)} %get-tuple-element.442, s32[128]{0:T(128)S(1)} %compare_select_fusion.9, f32[128,128,256]{2,1,0:T(8,128)} %convolution_multiply_fusion.5), kind=kCustom, calls=%fused_computation.3.clone.1 | custom fusion | flops 4194304 | bytes 50332160 | tf_op jit(solution)/shard_map/while/body/eval_jaxpr/scatter-add | solution.py:27
  679.0 71.8 %reduce-scatter.5.cloned.1.call-done = f32[512,256]{1,0:T(8,128)} async-done(((f32[8192,256]{1,0:T(8,128)}), f32[512,256]{1,0:T(8,128)}) %reduce-scatter.5.cloned.1.call-update) | async-done | bytes 524304 | tf_op jit(solution)/shard_map/reduce_scatter | solution.py:65
  754.9 144.8 %all-reduce.2.cloned.1.call-done = f32[256,256]{0,1:T(8,128)} async-done(((f32[256,256]{0,1:T(8,128)}), f32[256,256]{0,1:T(8,128)}) %all-reduce.2.cloned.1.call-update) | async-done | bytes 262160 | tf_op jit(solution)/shard_map/psum | solution.py:72
  (50 shorter events, 29.9 us)
Async XLA Ops:
  7.2 1.0 copy-start
  7.2 44.2 %all-gather.3.cloned.1.call-start = ((), (), s32[]{:S(2)}) async-start(), calls=%async_computation.2 | async-start | bytes 4456448 | tf_op jit(solution)/shard_map/all_gather | solution.py:47
  10.0 371.3 %reduce-scatter.3.cloned.1.call-start = ((), (), s32[]{:S(2)}) async-start(), calls=%async_computation.3 | async-start | bytes 4718592 | tf_op jit(solution)/shard_map/reduce_scatter | solution.py:51
  53.8 327.5 %copy-start.3 = (bf16[512,256]{1,0:T(8,128)(2,1)S(1)}, bf16[512,256]{1,0:T(8,128)(2,1)}, u32[]{:S(2)}) copy-start(bf16[512,256]{1,0:T(8,128)(2,1)} %param.13) | copy-start | bytes 786436
  298.0 139.9 %all-gather.5.cloned.1.call-start = ((), (), s32[]{:S(2)}) async-start(), calls=%async_computation.4 | async-start | bytes 2359296 | tf_op jit(solution)/shard_map/all_gather | solution.py:54
  383.4 367.4 %reduce-scatter.5.cloned.1.call-start = ((), (), s32[]{:S(2)}) async-start(), calls=%async_computation.5 | async-start | bytes 8912896 | tf_op jit(solution)/shard_map/reduce_scatter | solution.py:65
  437.9 4.2 copy-start.1
  679.0 73.9 %copy-start.2 = (bf16[256,256]{1,0:T(8,128)(2,1)S(1)}, bf16[256,256]{1,0:T(8,128)(2,1)}, u32[]{:S(2)}) copy-start(bf16[256,256]{1,0:T(8,128)(2,1)} %param.12) | copy-start | bytes 393220
  679.0 220.6 %all-reduce.2.cloned.1.call-start = ((), (), s32[]{:S(2)}) async-start(), calls=%async_computation.6 | async-start | bytes 524288 | tf_op jit(solution)/shard_map/psum | solution.py:72
Sparse Core Ops, SparseCore 0:
  10.3 41.0 all-gather.2
  298.1 83.1 reduce-scatter.2
  384.2 53.6 all-gather.4
  679.1 71.6 reduce-scatter.4
  756.0 143.6 all-reduce.1
where the time goes:
time: 910 us; the launch traced here: 908 us
  waiting for transfers between devices  372 us (41%)
  other arithmetic  319 us (35%)
  matrix products  108 us (12%)
  local copies, waits for them, and re-layouts  93.1 us (10%)
  between operations  14.5 us (2%)
    scatter-add x8, other arithmetic, accumulate(): return summed.at[places].add(products)  305 us
    psum x1, waiting for transfers between devices, body(): grad_weight = lax.psum(local_weight, ('dom', 'rep'))  145 us
    dot_general x8, matrix products, accumulate(): jnp.einsum(pattern, block_values, picked, preferred_element_type=jnp.floa...  103 us
    reduce_scatter x1, waiting for transfers between devices, body(): lax.psum_scatter(partial_value, 'rep', scatter_dimension=0, tiled=True)  83.2 us
    reduce_scatter x1, waiting for transfers between devices, body(): lax.psum_scatter(back_partial, 'dom', scatter_dimension=0, tiled=True)  71.8 us
    gather x8, local copies, waits for them, and re-layouts, accumulate(): picked = jnp.take(source, picks, axis=0)  61.3 us
    all_gather x1, waiting for transfers between devices, body(): gathered = lax.all_gather(projected, 'dom', axis=0, tiled=True)  40.7 us
    all_gather x1, waiting for transfers between devices, body(): grad_block = lax.all_gather(grad_own, 'rep', axis=0, tiled=True)  31.9 us
  transfers between devices with their start and end apart: 5, of which 5 were waited for; matrix products, arithmetic and copies ran while one was open for 3% of the time, Pallas kernels for 0%

commit v1 on v0

--- a/solution.py
+++ b/solution.py
@@ -69,7 +69,9 @@
         jnp.bfloat16
     )
     local_weight = jnp.dot(node_features.T, grad_projected, preferred_element_type=jnp.float32)
-    grad_weight = lax.psum(local_weight, ("dom", "rep"))
+    grad_weight = local_weight
+    for at in ("rep", "dom"):
+        grad_weight = lax.psum(grad_weight, at)
     return (output, grad_features, grad_weight)
 
 

time: 910 us -> 968 us (1.064)
  waiting for transfers between devices: 372 us -> 430 us
    psum x1 -> x2, waiting for transfers between devices: 145 us -> 202 us  [body(): grad_weight = lax.psum(grad_weight, at)]
  transfers between devices with their start and end apart: 5 -> 6, of which waited for: 5 -> 6; matrix products, arithmetic and copies ran while one was open for 3% -> 3% of each run, Pallas kernels for 0% -> 0%
where the time goes in v1:
time: 968 us; the launch traced here: 966 us
  waiting for transfers between devices  430 us (44%)
  other arithmetic  319 us (33%)
  matrix products  108 us (11%)
  local copies, waits for them, and re-layouts  93.1 us (10%)
  between operations  14.8 us (2%)
    scatter-add x8, other arithmetic, accumulate(): return summed.at[places].add(products)  305 us
    psum x2, waiting for transfers between devices, body(): grad_weight = lax.psum(grad_weight, at)  202 us
    dot_general x8, matrix products, accumulate(): jnp.einsum(pattern, block_values, picked, preferred_element_type=jnp.floa...  103 us
    reduce_scatter x1, waiting for transfers between devices, body(): lax.psum_scatter(partial_value, 'rep', scatter_dimension=0, tiled=True)  83.2 us
    reduce_scatter x1, waiting for transfers between devices, body(): lax.psum_scatter(back_partial, 'dom', scatter_dimension=0, tiled=True)  71.8 us
    gather x8, local copies, waits for them, and re-layouts, accumulate(): picked = jnp.take(source, picks, axis=0)  61.3 us
    all_gather x1, waiting for transfers between devices, body(): gathered = lax.all_gather(projected, 'dom', axis=0, tiled=True)  40.7 us
    all_gather x1, waiting for transfers between devices, body(): grad_block = lax.all_gather(grad_own, 'rep', axis=0, tiled=True)  31.9 us
  transfers between devices with their start and end apart: 6, of which 6 were waited for; matrix products, arithmetic and copies ran while one was open for 3% of the time, Pallas kernels for 0%

profile of v1, /device:TPU:1, one launch (start us, length us, event | category | flops | bytes accessed | tf_op | source)
XLA Modules:
  0.0 965.9 jit_solution(5782684220008788407)
XLA Ops:
  10.7 40.7 %all-gather.3.cloned.1.call-done = bf16[8192,256]{1,0:T(8,128)(2,1)} async-done(((bf16[512,256]{1,0:T(8,128)(2,1)}), bf16[8192,256]{1,0:T(8,128)(2,1)}) %all-gather.3.cloned.1.call-update) | async-done | bytes 4194320 | tf_op jit(solution)/shard_map/all_gather | solution.py:47
  53.8 244.2 %while.26 = (s32[]{:T(128)}, f32[32,128,256]{2,1,0:T(8,128)}, s32[512]{0:T(512)}, bf16[512,128,128]{2,1,0:T(8,128)(2,1)}, s32[512]{0:T(512)}, /*index=5*/bf16[64...) while((s32[]{:T(128)}, f32[32,128,256]{2,1,0:T(8,128)}, ...), condition=%wide.region_2.3_spmd, body=%wide.region_0.2_spmd.sunk | while | flops 1086327040 | bytes 96478248 | solution.py:30
  54.6 8.8 gather_fusion
  63.4 12.8 %convolution_multiply_fusion.4 = f32[128,128,256]{2,1,0:T(8,128)} fusion(f32[128]{0:T(128)S(1)} %get-tuple-element.384, bf16[128,128,256]{2,1,0:T(8,128)(2,1)} %gather_fusion, pred[128]{0:T(512)(128)(4,1)S(1)} %get-tuple-element.386, bf16[512,128,128]{2,1,0:T(8,128)(2,1)} %get-tuple-element.422, s32[]{:T(128)S(6)} %select_n.85), kind=kOutput, calls=%fused_computation.4.clone.1 | convolution fusion | flops 1082130432 | bytes 29360772 | tf_op jit(solution)/shard_map/while/body/eval_jaxpr/tab,tbf->taf/dot_general | solution.py:23
  76.9 38.1 %scatter_fusion = f32[32,128,256]{2,1,0:T(8,128)} fusion(f32[32,128,256]{2,1,0:T(8,128)} %get-tuple-element.409, s32[128]{0:T(128)S(1)} %compare_select_fusion.8, f32[128,128,256]{2,1,0:T(8,128)} %convolution_multiply_fusion.4), kind=kCustom, calls=%fused_computation.2.clone.1 | custom fusion | flops 4194304 | bytes 50332160 | tf_op jit(solution)/shard_map/while/body/eval_jaxpr/scatter-add | solution.py:27
  115.8 8.8 gather_fusion
  124.5 12.8 %convolution_multiply_fusion.4 = f32[128,128,256]{2,1,0:T(8,128)} fusion(f32[128]{0:T(128)S(1)} %get-tuple-element.384, bf16[128,128,256]{2,1,0:T(8,128)(2,1)} %gather_fusion, pred[128]{0:T(512)(128)(4,1)S(1)} %get-tuple-element.386, bf16[512,128,128]{2,1,0:T(8,128)(2,1)} %get-tuple-element.422, s32[]{:T(128)S(6)} %select_n.85), kind=kOutput, calls=%fused_computation.4.clone.1 | convolution fusion | flops 1082130432 | bytes 29360772 | tf_op jit(solution)/shard_map/while/body/eval_jaxpr/tab,tbf->taf/dot_general | solution.py:23
  138.1 38.1 %scatter_fusion = f32[32,128,256]{2,1,0:T(8,128)} fusion(f32[32,128,256]{2,1,0:T(8,128)} %get-tuple-element.409, s32[128]{0:T(128)S(1)} %compare_select_fusion.8, f32[128,128,256]{2,1,0:T(8,128)} %convolution_multiply_fusion.4), kind=kCustom, calls=%fused_computation.2.clone.1 | custom fusion | flops 4194304 | bytes 50332160 | tf_op jit(solution)/shard_map/while/body/eval_jaxpr/scatter-add | solution.py:27
  176.9 8.8 gather_fusion
  185.7 12.8 %convolution_multiply_fusion.4 = f32[128,128,256]{2,1,0:T(8,128)} fusion(f32[128]{0:T(128)S(1)} %get-tuple-element.384, bf16[128,128,256]{2,1,0:T(8,128)(2,1)} %gather_fusion, pred[128]{0:T(512)(128)(4,1)S(1)} %get-tuple-element.386, bf16[512,128,128]{2,1,0:T(8,128)(2,1)} %get-tuple-element.422, s32[]{:T(128)S(6)} %select_n.85), kind=kOutput, calls=%fused_computation.4.clone.1 | convolution fusion | flops 1082130432 | bytes 29360772 | tf_op jit(solution)/shard_map/while/body/eval_jaxpr/tab,tbf->taf/dot_general | solution.py:23
  199.3 37.7 %scatter_fusion = f32[32,128,256]{2,1,0:T(8,128)} fusion(f32[32,128,256]{2,1,0:T(8,128)} %get-tuple-element.409, s32[128]{0:T(128)S(1)} %compare_select_fusion.8, f32[128,128,256]{2,1,0:T(8,128)} %convolution_multiply_fusion.4), kind=kCustom, calls=%fused_computation.2.clone.1 | custom fusion | flops 4194304 | bytes 50332160 | tf_op jit(solution)/shard_map/while/body/eval_jaxpr/scatter-add | solution.py:27
  237.7 8.8 gather_fusion
  246.5 12.8 %convolution_multiply_fusion.4 = f32[128,128,256]{2,1,0:T(8,128)} fusion(f32[128]{0:T(128)S(1)} %get-tuple-element.384, bf16[128,128,256]{2,1,0:T(8,128)(2,1)} %gather_fusion, pred[128]{0:T(512)(128)(4,1)S(1)} %get-tuple-element.386, bf16[512,128,128]{2,1,0:T(8,128)(2,1)} %get-tuple-element.422, s32[]{:T(128)S(6)} %select_n.85), kind=kOutput, calls=%fused_computation.4.clone.1 | convolution fusion | flops 1082130432 | bytes 29360772 | tf_op jit(solution)/shard_map/while/body/eval_jaxpr/tab,tbf->taf/dot_general | solution.py:23
  260.1 37.9 %scatter_fusion = f32[32,128,256]{2,1,0:T(8,128)} fusion(f32[32,128,256]{2,1,0:T(8,128)} %get-tuple-element.409, s32[128]{0:T(128)S(1)} %compare_select_fusion.8, f32[128,128,256]{2,1,0:T(8,128)} %convolution_multiply_fusion.4), kind=kCustom, calls=%fused_computation.2.clone.1 | custom fusion | flops 4194304 | bytes 50332160 | tf_op jit(solution)/shard_map/while/body/eval_jaxpr/scatter-add | solution.py:27
  298.0 83.2 %reduce-scatter.3.cloned.1.call-done = f32[512,256]{1,0:T(8,128)} async-done(((f32[4096,256]{1,0:T(8,128)}), f32[512,256]{1,0:T(8,128)}) %reduce-scatter.3.cloned.1.call-update) | async-done | bytes 524304 | tf_op jit(solution)/shard_map/reduce_scatter | solution.py:51
  383.6 22.4 %copy.10 = bf16[1,1,512,128,128]{3,4,2,1,0:T(8,128)(2,1)} copy(bf16[1,1,512,128,128]{4,3,2,1,0:T(8,128)(2,1)} %bitcast.21) | data formatting | bytes 33554432 | tf_op args[5]
  406.0 31.9 %all-gather.5.cloned.1.call-done = bf16[4096,256]{1,0:T(8,128)(2,1)} async-done(((bf16[512,256]{1,0:T(8,128)(2,1)}), bf16[4096,256]{1,0:T(8,128)(2,1)}) %all-gather.5.cloned.1.call-update) | async-done | bytes 2097168 | tf_op jit(solution)/shard_map/all_gather | solution.py:54
  442.1 236.8 %while.27 = (s32[]{:T(128)}, f32[64,128,256]{2,1,0:T(8,128)}, s32[512]{0:T(512)}, bf16[512,128,128]{1,2,0:T(8,128)(2,1)}, s32[512]{0:T(512)}, /*index=5*/bf16[32...) while((s32[]{:T(128)}, f32[64,128,256]{2,1,0:T(8,128)}, ...), condition=%wide.region_6.7_spmd, body=%wide.region_4.6_spmd.sunk | while | flops 1086327040 | bytes 96478248 | solution.py:30
  442.9 6.6 gather_fusion.1
  449.5 12.8 %convolution_multiply_fusion.5 = f32[128,128,256]{2,1,0:T(8,128)} fusion(f32[128]{0:T(128)S(1)} %get-tuple-element.394, bf16[128,128,256]{2,1,0:T(8,128)(2,1)} %gather_fusion.1, pred[128]{0:T(512)(128)(4,1)S(1)} %get-tuple-element.396, bf16[512,128,128]{1,2,0:T(8,128)(2,1)} %get-tuple-element.455, s32[]{:T(128)S(6)} %select_n.88), kind=kOutput, calls=%fused_computation.16.clone.1 | convolution fusion | flops 1082130432 | bytes 29360772 | tf_op jit(solution)/shard_map/while/body/eval_jaxpr/tba,tbf->taf/dot_general | solution.py:23
  463.1 38.5 %scatter_fusion.1 = f32[64,128,256]{2,1,0:T(8,128)} fusion(f32[64,128,256]{2,1,0:T(8,128)} %get-tuple-element.442, s32[128]{0:T(128)S(1)} %compare_select_fusion.9, f32[128,128,256]{2,1,0:T(8,128)} %convolution_multiply_fusion.5), kind=kCustom, calls=%fused_computation.3.clone.1 | custom fusion | flops 4194304 | bytes 50332160 | tf_op jit(solution)/shard_map/while/body/eval_jaxpr/scatter-add | solution.py:27
  508.9 12.8 %convolution_multiply_fusion.5 = f32[128,128,256]{2,1,0:T(8,128)} fusion(f32[128]{0:T(128)S(1)} %get-tuple-element.394, bf16[128,128,256]{2,1,0:T(8,128)(2,1)} %gather_fusion.1, pred[128]{0:T(512)(128)(4,1)S(1)} %get-tuple-element.396, bf16[512,128,128]{1,2,0:T(8,128)(2,1)} %get-tuple-element.455, s32[]{:T(128)S(6)} %select_n.88), kind=kOutput, calls=%fused_computation.16.clone.1 | convolution fusion | flops 1082130432 | bytes 29360772 | tf_op jit(solution)/shard_map/while/body/eval_jaxpr/tba,tbf->taf/dot_general | solution.py:23
  522.5 38.1 %scatter_fusion.1 = f32[64,128,256]{2,1,0:T(8,128)} fusion(f32[64,128,256]{2,1,0:T(8,128)} %get-tuple-element.442, s32[128]{0:T(128)S(1)} %compare_select_fusion.9, f32[128,128,256]{2,1,0:T(8,128)} %convolution_multiply_fusion.5), kind=kCustom, calls=%fused_computation.3.clone.1 | custom fusion | flops 4194304 | bytes 50332160 | tf_op jit(solution)/shard_map/while/body/eval_jaxpr/scatter-add | solution.py:27
  561.3 6.6 gather_fusion.1
  567.9 12.8 %convolution_multiply_fusion.5 = f32[128,128,256]{2,1,0:T(8,128)} fusion(f32[128]{0:T(128)S(1)} %get-tuple-element.394, bf16[128,128,256]{2,1,0:T(8,128)(2,1)} %gather_fusion.1, pred[128]{0:T(512)(128)(4,1)S(1)} %get-tuple-element.396, bf16[512,128,128]{1,2,0:T(8,128)(2,1)} %get-tuple-element.455, s32[]{:T(128)S(6)} %select_n.88), kind=kOutput, calls=%fused_computation.16.clone.1 | convolution fusion | flops 1082130432 | bytes 29360772 | tf_op jit(solution)/shard_map/while/body/eval_jaxpr/tba,tbf->taf/dot_general | solution.py:23
  581.5 38.3 %scatter_fusion.1 = f32[64,128,256]{2,1,0:T(8,128)} fusion(f32[64,128,256]{2,1,0:T(8,128)} %get-tuple-element.442, s32[128]{0:T(128)S(1)} %compare_select_fusion.9, f32[128,128,256]{2,1,0:T(8,128)} %convolution_multiply_fusion.5), kind=kCustom, calls=%fused_computation.3.clone.1 | custom fusion | flops 4194304 | bytes 50332160 | tf_op jit(solution)/shard_map/while/body/eval_jaxpr/scatter-add | solution.py:27
  620.5 6.6 gather_fusion.1
  627.1 12.8 %convolution_multiply_fusion.5 = f32[128,128,256]{2,1,0:T(8,128)} fusion(f32[128]{0:T(128)S(1)} %get-tuple-element.394, bf16[128,128,256]{2,1,0:T(8,128)(2,1)} %gather_fusion.1, pred[128]{0:T(512)(128)(4,1)S(1)} %get-tuple-element.396, bf16[512,128,128]{1,2,0:T(8,128)(2,1)} %get-tuple-element.455, s32[]{:T(128)S(6)} %select_n.88), kind=kOutput, calls=%fused_computation.16.clone.1 | convolution fusion | flops 1082130432 | bytes 29360772 | tf_op jit(solution)/shard_map/while/body/eval_jaxpr/tba,tbf->taf/dot_general | solution.py:23
  640.7 38.3 %scatter_fusion.1 = f32[64,128,256]{2,1,0:T(8,128)} fusion(f32[64,128,256]{2,1,0:T(8,128)} %get-tuple-element.442, s32[128]{0:T(128)S(1)} %compare_select_fusion.9, f32[128,128,256]{2,1,0:T(8,128)} %convolution_multiply_fusion.5), kind=kCustom, calls=%fused_computation.3.clone.1 | custom fusion | flops 4194304 | bytes 50332160 | tf_op jit(solution)/shard_map/while/body/eval_jaxpr/scatter-add | solution.py:27
  679.1 71.8 %reduce-scatter.5.cloned.1.call-done = f32[512,256]{1,0:T(8,128)} async-done(((f32[8192,256]{1,0:T(8,128)}), f32[512,256]{1,0:T(8,128)}) %reduce-scatter.5.cloned.1.call-update) | async-done | bytes 524304 | tf_op jit(solution)/shard_map/reduce_scatter | solution.py:65
  752.9 81.8 %all-reduce.3.cloned.1.call-done = f32[256,256]{0,1:T(8,128)} async-done(((f32[256,256]{0,1:T(8,128)}), f32[256,256]{0,1:T(8,128)}) %all-reduce.3.cloned.1.call-update) | async-done | bytes 262160 | tf_op jit(solution)/shard_map/psum | solution.py:74
  836.8 120.5 %all-reduce.5.cloned.1.call-done = f32[256,256]{0,1:T(8,128)} async-done(((f32[256,256]{0,1:T(8,128)}), f32[256,256]{0,1:T(8,128)}) %all-reduce.5.cloned.1.call-update) | async-done | bytes 262160 | tf_op jit(solution)/shard_map/psum | solution.py:74
  (53 shorter events, 36.5 us)
Async XLA Ops:
  7.2 1.0 copy-start
  7.2 44.2 %all-gather.3.cloned.1.call-start = ((), (), s32[]{:S(2)}) async-start(), calls=%async_computation.2 | async-start | bytes 4456448 | tf_op jit(solution)/shard_map/all_gather | solution.py:47
  10.0 371.3 %reduce-scatter.3.cloned.1.call-start = ((), (), s32[]{:S(2)}) async-start(), calls=%async_computation.3 | async-start | bytes 4718592 | tf_op jit(solution)/shard_map/reduce_scatter | solution.py:51
  53.8 327.5 %copy-start.3 = (bf16[512,256]{1,0:T(8,128)(2,1)S(1)}, bf16[512,256]{1,0:T(8,128)(2,1)}, u32[]{:S(2)}) copy-start(bf16[512,256]{1,0:T(8,128)(2,1)} %param.13) | copy-start | bytes 786436
  298.0 139.9 %all-gather.5.cloned.1.call-start = ((), (), s32[]{:S(2)}) async-start(), calls=%async_computation.4 | async-start | bytes 2359296 | tf_op jit(solution)/shard_map/all_gather | solution.py:54
  383.4 367.4 %reduce-scatter.5.cloned.1.call-start = ((), (), s32[]{:S(2)}) async-start(), calls=%async_computation.5 | async-start | bytes 8912896 | tf_op jit(solution)/shard_map/reduce_scatter | solution.py:65
  437.9 4.2 copy-start.1
  679.0 155.8 %copy-start.2 = (bf16[256,256]{1,0:T(8,128)(2,1)S(1)}, bf16[256,256]{1,0:T(8,128)(2,1)}, u32[]{:S(2)}) copy-start(bf16[256,256]{1,0:T(8,128)(2,1)} %param.12) | copy-start | bytes 393220
  679.0 155.7 %all-reduce.3.cloned.1.call-start = ((), (), s32[]{:S(2)}) async-start(), calls=%async_computation.6 | async-start | bytes 524288 | tf_op jit(solution)/shard_map/psum | solution.py:74
  752.8 204.4 %all-reduce.5.cloned.1.call-start = ((), (), s32[]{:S(2)}) async-start(), calls=%async_computation.7 | async-start | bytes 524288 | tf_op jit(solution)/shard_map/psum | solution.py:74
Sparse Core Ops, SparseCore 0:
  10.3 41.0 all-gather.2
  298.1 83.1 reduce-scatter.2
  384.2 53.6 all-gather.4
  679.1 71.6 reduce-scatter.4
  753.7 80.9 all-reduce.2
  837.2 120.0 all-reduce.4
